TPU v7x, 256 devices: a whole 4x4x8 slice. The times are simulated.
256 devices in a mesh: row: 16 (over y, x), col: 16 (over z, core).
Axes of the slice: x: 4, y: 4, z: 8, core: 2. Of those that a mesh axis runs over, the one named last changes fastest.
Arguments:
- right_side: float32 [8192, 8192], P('row', 'col'), may hold values from -6 to 6
- upper_left: bfloat16 [8192, 8192], P('row', 'col'), may hold values from -0.1875 to 0.1875
- upper_right: bfloat16 [8192, 8192], P('row', 'col'), may hold values from -0.1875 to 0.1875
- vectors_left: bfloat16 [8192, 512], P('row'), may hold values from -1 to 1, as said below
- vectors_right: bfloat16 [8192, 512], P('col'), may hold values from -1 to 1, as said below
- values_left: float32 [8192], P('row'), may hold values from 0.5 to 1
- values_right: float32 [8192], P('col'), may hold values from 0.5 to 1
Outputs:
- progress: float32 [8192, 8192], P('row', 'col')
Inputs may be any that keep to these rules, and one draw needn't show every extreme that they name: `vectors_left`: each block of 512 rows is an orthogonal matrix rounded to bfloat16. `vectors_right`: each block of 512 rows is an orthogonal matrix rounded to bfloat16.
All inputs are finite; a program needn't handle non-finite values.
Results may differ from a plain program's by a relative error of at most 0.023.
Values may be sent and summed in bfloat16 or wider, within the bound.
A program may use at most 128 MiB of HBM per device.

v0:
```python
import jax
import jax.numpy as jnp
from jax import lax
from jax.sharding import PartitionSpec as P

STEPS = 8


def from_root(array, axis, root):
    return lax.dynamic_index_in_dim(lax.all_gather(array, axis), root, 0, keepdims=False)


def solve_tile(remain, vec_left, vec_right, eigen_sums):
    halfway = lax.dot_general(
        vec_left,
        remain.astype(jnp.bfloat16),
        (((0,), (0,)), ((), ())),
        preferred_element_type=jnp.float32,
    ).astype(jnp.bfloat16)
    rotated = jnp.dot(halfway, vec_right, preferred_element_type=jnp.float32)
    scaled = (rotated / eigen_sums).astype(jnp.bfloat16)
    turned = jnp.dot(vec_left, scaled, preferred_element_type=jnp.float32).astype(jnp.bfloat16)
    return lax.dot_general(
        turned, vec_right, (((1,), (1,)), ((), ())), preferred_element_type=jnp.float32
    )


def per_device(
    right_side, upper_left, upper_right, vectors_left, vectors_right, values_left, values_right
):
    row_count = lax.axis_size("row")
    col_count = lax.axis_size("col")
    my_row = lax.axis_index("row")
    my_col = lax.axis_index("col")
    tile_size = right_side.shape[0]
    left_block = lax.all_gather(upper_left, "col", axis=1, tiled=True)
    right_block = lax.all_gather(upper_right, "row", axis=0, tiled=True)
    eigen_sums = values_left[:, None] + values_right[None, :]
    row_lag = row_count - 1 - my_row
    current = right_side
    for section_index in range(STEPS):
        ready = row_lag + my_col == section_index

        def run_solve(remain):
            return solve_tile(remain, vectors_left, vectors_right, eigen_sums)

        def skip_solve(remain):
            return jnp.zeros_like(remain)

        answer = lax.cond(ready, run_solve, skip_solve, current)
        current = jnp.where(ready, answer, current)
        rounded = answer.astype(jnp.bfloat16)
        source_lag = section_index - my_col
        column_valid = jnp.logical_and(source_lag >= 0, source_lag < row_count)
        source_row = jnp.clip(row_count - 1 - source_lag, 0, row_count - 1)
        column_mask = jnp.where(
            jnp.logical_and(column_valid, my_row < source_row), 1.0, 0.0
        ).astype(jnp.float32)
        source_col_raw = section_index - row_lag
        row_valid = jnp.logical_and(source_col_raw >= 0, source_col_raw < col_count)
        source_col = jnp.clip(source_col_raw, 0, col_count - 1)
        row_mask = jnp.where(jnp.logical_and(row_valid, my_col > source_col), 1.0, 0.0).astype(
            jnp.float32
        )
        from_below = from_root(rounded, "row", source_row)
        from_left = from_root(rounded, "col", source_col)
        left_tile = lax.dynamic_slice_in_dim(left_block, source_row * tile_size, tile_size, 1)
        right_tile = lax.dynamic_slice_in_dim(right_block, source_col * tile_size, tile_size, 0)
        column_update = jnp.dot(left_tile, from_below, preferred_element_type=jnp.float32)
        row_update = jnp.dot(from_left, right_tile, preferred_element_type=jnp.float32)
        current = current - column_mask * column_update - row_mask * row_update
    return current


def solution(mesh):
    in_specs = (
        P("row", "col"),
        P("row", "col"),
        P("row", "col"),
        P("row", None),
        P("col", None),
        P("row"),
        P("col"),
    )
    out_specs = P("row", "col")
    return jax.shard_map(
        per_device, mesh=mesh, in_specs=in_specs, out_specs=out_specs, check_vma=False
    )
```

profile of v0, /device:TPU:2, one launch (start us, length us, event | category | flops | bytes accessed | tf_op | source)
XLA Modules:
  0.0 1256.5 jit_solution(16066382461646001978)
XLA Ops:
  7.4 1.2 conditional.8
  7.4 1.1 broadcast.50
  11.5 77.0 %all-gather.21.cloned.1.call-done = bf16[16,512,512]{2,1,0:T(8,128)(2,1)} async-done(((bf16[1,512,512]{2,1,0:T(8,128)(2,1)}), bf16[16,512,512]{2,1,0:T(8,128)(2,1)}) %all-gather.21.cloned.1.call-update) | async-done | bytes 8388624 | tf_op jit(solution)/shard_map/all_gather | solution.py:10
  88.6 57.5 %all-gather.19.cloned.1.call-done = bf16[512,8192]{1,0:T(8,128)(2,1)} async-done(((bf16[512,512]{1,0:T(8,128)(2,1)}), bf16[512,8192]{1,0:T(8,128)(2,1)}) %all-gather.19.cloned.1.call-update) | async-done | bytes 8388624 | tf_op jit(solution)/shard_map/all_gather | solution.py:36
  146.0 2.0 fusion.47
  148.0 54.3 %all-gather.23.cloned.1.call-done = bf16[16,512,512]{2,1,0:T(8,128)(2,1)} async-done(((bf16[1,512,512]{2,1,0:T(8,128)(2,1)}), bf16[16,512,512]{2,1,0:T(8,128)(2,1)}) %all-gather.23.cloned.1.call-update) | async-done | bytes 8388624 | tf_op jit(solution)/shard_map/all_gather | solution.py:10
  202.3 76.7 %all-gather.25.cloned.1.call-done = bf16[8192,512]{1,0:T(8,128)(2,1)} async-done(((bf16[512,512]{1,0:T(8,128)(2,1)}), bf16[8192,512]{1,0:T(8,128)(2,1)}) %all-gather.25.cloned.1.call-update) | async-done | bytes 8388624 | tf_op jit(solution)/shard_map/all_gather | solution.py:37
  279.0 1.6 fusion.46
  280.6 1.2 conditional.9
  280.6 1.1 broadcast.51
  283.3 75.0 %all-gather.27.cloned.1.call-done = bf16[16,512,512]{2,1,0:T(8,128)(2,1)} async-done(((bf16[1,512,512]{2,1,0:T(8,128)(2,1)}), bf16[16,512,512]{2,1,0:T(8,128)(2,1)}) %all-gather.27.cloned.1.call-update) | async-done | bytes 8388624 | tf_op jit(solution)/shard_map/all_gather | solution.py:10
  358.3 1.6 fusion.45
  360.0 55.7 %all-gather.29.cloned.1.call-done = bf16[16,512,512]{2,1,0:T(8,128)(2,1)} async-done(((bf16[1,512,512]{2,1,0:T(8,128)(2,1)}), bf16[16,512,512]{2,1,0:T(8,128)(2,1)}) %all-gather.29.cloned.1.call-update) | async-done | bytes 8388624 | tf_op jit(solution)/shard_map/all_gather | solution.py:10
  415.6 1.6 fusion.44
  417.3 1.2 conditional.10
  417.3 1.1 broadcast.52
  420.1 76.0 %all-gather.31.cloned.1.call-done = bf16[16,512,512]{2,1,0:T(8,128)(2,1)} async-done(((bf16[1,512,512]{2,1,0:T(8,128)(2,1)}), bf16[16,512,512]{2,1,0:T(8,128)(2,1)}) %all-gather.31.cloned.1.call-update) | async-done | bytes 8388624 | tf_op jit(solution)/shard_map/all_gather | solution.py:10
  496.1 1.6 fusion.43
  497.8 55.8 %all-gather.33.cloned.1.call-done = bf16[16,512,512]{2,1,0:T(8,128)(2,1)} async-done(((bf16[1,512,512]{2,1,0:T(8,128)(2,1)}), bf16[16,512,512]{2,1,0:T(8,128)(2,1)}) %all-gather.33.cloned.1.call-update) | async-done | bytes 8388624 | tf_op jit(solution)/shard_map/all_gather | solution.py:10
  553.6 1.6 fusion.42
  555.2 1.2 conditional.11
  555.2 1.1 broadcast.53
  557.9 75.4 %all-gather.35.cloned.1.call-done = bf16[16,512,512]{2,1,0:T(8,128)(2,1)} async-done(((bf16[1,512,512]{2,1,0:T(8,128)(2,1)}), bf16[16,512,512]{2,1,0:T(8,128)(2,1)}) %all-gather.35.cloned.1.call-update) | async-done | bytes 8388624 | tf_op jit(solution)/shard_map/all_gather | solution.py:10
  633.3 1.6 fusion.41
  635.0 55.6 %all-gather.37.cloned.1.call-done = bf16[16,512,512]{2,1,0:T(8,128)(2,1)} async-done(((bf16[1,512,512]{2,1,0:T(8,128)(2,1)}), bf16[16,512,512]{2,1,0:T(8,128)(2,1)}) %all-gather.37.cloned.1.call-update) | async-done | bytes 8388624 | tf_op jit(solution)/shard_map/all_gather | solution.py:10
  690.6 1.6 fusion.40
  692.3 1.2 conditional.12
  692.3 1.1 broadcast.54
  694.9 76.3 %all-gather.39.cloned.1.call-done = bf16[16,512,512]{2,1,0:T(8,128)(2,1)} async-done(((bf16[1,512,512]{2,1,0:T(8,128)(2,1)}), bf16[16,512,512]{2,1,0:T(8,128)(2,1)}) %all-gather.39.cloned.1.call-update) | async-done | bytes 8388624 | tf_op jit(solution)/shard_map/all_gather | solution.py:10
  771.2 1.6 fusion.39
  772.9 55.7 %all-gather.41.cloned.1.call-done = bf16[16,512,512]{2,1,0:T(8,128)(2,1)} async-done(((bf16[1,512,512]{2,1,0:T(8,128)(2,1)}), bf16[16,512,512]{2,1,0:T(8,128)(2,1)}) %all-gather.41.cloned.1.call-update) | async-done | bytes 8388624 | tf_op jit(solution)/shard_map/all_gather | solution.py:10
  828.5 1.6 fusion.38
  830.2 1.3 conditional.13
  830.2 1.1 broadcast.55
  833.0 76.6 %all-gather.43.cloned.1.call-done = bf16[16,512,512]{2,1,0:T(8,128)(2,1)} async-done(((bf16[1,512,512]{2,1,0:T(8,128)(2,1)}), bf16[16,512,512]{2,1,0:T(8,128)(2,1)}) %all-gather.43.cloned.1.call-update) | async-done | bytes 8388624 | tf_op jit(solution)/shard_map/all_gather | solution.py:10
  909.6 1.6 fusion.37
  911.2 55.7 %all-gather.45.cloned.1.call-done = bf16[16,512,512]{2,1,0:T(8,128)(2,1)} async-done(((bf16[1,512,512]{2,1,0:T(8,128)(2,1)}), bf16[16,512,512]{2,1,0:T(8,128)(2,1)}) %all-gather.45.cloned.1.call-update) | async-done | bytes 8388624 | tf_op jit(solution)/shard_map/all_gather | solution.py:10
  966.9 1.6 fusion.36
  968.5 1.2 conditional.14
  971.2 78.3 %all-gather.47.cloned.1.call-done = bf16[16,512,512]{2,1,0:T(8,128)(2,1)} async-done(((bf16[1,512,512]{2,1,0:T(8,128)(2,1)}), bf16[16,512,512]{2,1,0:T(8,128)(2,1)}) %all-gather.47.cloned.1.call-update) | async-done | bytes 8388624 | tf_op jit(solution)/shard_map/all_gather | solution.py:10
  1049.5 1.6 fusion.35
  1051.2 55.7 %all-gather.49.cloned.1.call-done = bf16[16,512,512]{2,1,0:T(8,128)(2,1)} async-done(((bf16[1,512,512]{2,1,0:T(8,128)(2,1)}), bf16[16,512,512]{2,1,0:T(8,128)(2,1)}) %all-gather.49.cloned.1.call-update) | async-done | bytes 8388624 | tf_op jit(solution)/shard_map/all_gather | solution.py:10
  1106.8 1.6 fusion.34
  1108.5 1.2 conditional.15
  1111.1 78.7 %all-gather.51.cloned.1.call-done = bf16[16,512,512]{2,1,0:T(8,128)(2,1)} async-done(((bf16[1,512,512]{2,1,0:T(8,128)(2,1)}), bf16[16,512,512]{2,1,0:T(8,128)(2,1)}) %all-gather.51.cloned.1.call-update) | async-done | bytes 8388624 | tf_op jit(solution)/shard_map/all_gather | solution.py:10
  1189.8 1.6 fusion.33
  1191.4 55.7 %all-gather.53.cloned.1.call-done = bf16[16,512,512]{2,1,0:T(8,128)(2,1)} async-done(((bf16[1,512,512]{2,1,0:T(8,128)(2,1)}), bf16[16,512,512]{2,1,0:T(8,128)(2,1)}) %all-gather.53.cloned.1.call-update) | async-done | bytes 8388624 | tf_op jit(solution)/shard_map/all_gather | solution.py:10
  1247.1 2.6 fusion.32
  (63 shorter events, 16.4 us)
Async XLA Ops:
  6.5 82.0 %all-gather.21.cloned.1.call-start = ((), (), s32[]{:S(2)}) async-start(), calls=%async_computation.1 | async-start | bytes 8912896 | tf_op jit(solution)/shard_map/all_gather | solution.py:10
  8.5 0.8 copy-start
  9.4 136.6 %all-gather.19.cloned.1.call-start = ((), (), s32[]{:S(2)}) async-start(), calls=%async_computation | async-start | bytes 8912896 | tf_op jit(solution)/shard_map/all_gather | solution.py:36
  10.1 192.1 %all-gather.23.cloned.1.call-start = ((), (), s32[]{:S(2)}) async-start(), calls=%async_computation.2 | async-start | bytes 8912896 | tf_op jit(solution)/shard_map/all_gather | solution.py:10
  10.9 268.1 %all-gather.25.cloned.1.call-start = ((), (), s32[]{:S(2)}) async-start(), calls=%async_computation.3 | async-start | bytes 8912896 | tf_op jit(solution)/shard_map/all_gather | solution.py:37
  11.5 346.9 %all-gather.27.cloned.1.call-start = ((), (), s32[]{:S(2)}) async-start(), calls=%async_computation.4 | async-start | bytes 8912896 | tf_op jit(solution)/shard_map/all_gather | solution.py:10
  281.8 0.8 copy-start.1
  282.6 133.0 %all-gather.29.cloned.1.call-start = ((), (), s32[]{:S(2)}) async-start(), calls=%async_computation.5 | async-start | bytes 8912896 | tf_op jit(solution)/shard_map/all_gather | solution.py:10
  283.2 212.9 %all-gather.31.cloned.1.call-start = ((), (), s32[]{:S(2)}) async-start(), calls=%async_computation.6 | async-start | bytes 8912896 | tf_op jit(solution)/shard_map/all_gather | solution.py:10
  418.4 0.8 copy-start.2
  419.3 134.3 %all-gather.33.cloned.1.call-start = ((), (), s32[]{:S(2)}) async-start(), calls=%async_computation.7 | async-start | bytes 8912896 | tf_op jit(solution)/shard_map/all_gather | solution.py:10
  420.0 213.3 %all-gather.35.cloned.1.call-start = ((), (), s32[]{:S(2)}) async-start(), calls=%async_computation.8 | async-start | bytes 8912896 | tf_op jit(solution)/shard_map/all_gather | solution.py:10
  556.4 0.8 copy-start.3
  557.2 133.4 %all-gather.37.cloned.1.call-start = ((), (), s32[]{:S(2)}) async-start(), calls=%async_computation.9 | async-start | bytes 8912896 | tf_op jit(solution)/shard_map/all_gather | solution.py:10
  557.8 213.4 %all-gather.39.cloned.1.call-start = ((), (), s32[]{:S(2)}) async-start(), calls=%async_computation.10 | async-start | bytes 8912896 | tf_op jit(solution)/shard_map/all_gather | solution.py:10
  693.4 0.8 copy-start.4
  694.3 134.2 %all-gather.41.cloned.1.call-start = ((), (), s32[]{:S(2)}) async-start(), calls=%async_computation.11 | async-start | bytes 8912896 | tf_op jit(solution)/shard_map/all_gather | solution.py:10
  694.9 214.7 %all-gather.43.cloned.1.call-start = ((), (), s32[]{:S(2)}) async-start(), calls=%async_computation.12 | async-start | bytes 8912896 | tf_op jit(solution)/shard_map/all_gather | solution.py:10
  831.5 0.8 copy-start.5
  832.3 134.5 %all-gather.45.cloned.1.call-start = ((), (), s32[]{:S(2)}) async-start(), calls=%async_computation.13 | async-start | bytes 8912896 | tf_op jit(solution)/shard_map/all_gather | solution.py:10
  832.9 216.6 %all-gather.47.cloned.1.call-start = ((), (), s32[]{:S(2)}) async-start(), calls=%async_computation.14 | async-start | bytes 8912896 | tf_op jit(solution)/shard_map/all_gather | solution.py:10
  969.7 0.8 copy-start.6
  970.5 136.3 %all-gather.49.cloned.1.call-start = ((), (), s32[]{:S(2)}) async-start(), calls=%async_computation.15 | async-start | bytes 8912896 | tf_op jit(solution)/shard_map/all_gather | solution.py:10
  971.1 218.7 %all-gather.51.cloned.1.call-start = ((), (), s32[]{:S(2)}) async-start(), calls=%async_computation.16 | async-start | bytes 8912896 | tf_op jit(solution)/shard_map/all_gather | solution.py:10
  1109.6 0.8 copy-start.7
  1110.5 136.6 %all-gather.53.cloned.1.call-start = ((), (), s32[]{:S(2)}) async-start(), calls=%async_computation.17 | async-start | bytes 8912896 | tf_op jit(solution)/shard_map/all_gather | solution.py:10
Sparse Core Ops, SparseCore 0:
  9.8 78.7 all-gather.20
  90.4 55.5 all-gather.18
  147.9 54.3 all-gather.22
  204.6 74.3 all-gather.24
  282.8 75.5 all-gather.26
  360.0 55.5 all-gather.28
  419.4 76.6 all-gather.30
  498.0 55.5 all-gather.32
  557.3 75.9 all-gather.34
  635.0 55.5 all-gather.36
  694.4 76.7 all-gather.38
  772.9 55.5 all-gather.40
  832.5 77.0 all-gather.42
  911.2 55.5 all-gather.44
  970.6 78.8 all-gather.46
  1051.2 55.5 all-gather.48
  1110.6 79.1 all-gather.50
  1191.5 55.5 all-gather.52
where the time goes:
time: 1260 us
  waiting for transfers between devices  1200 us (95%)
  matrix products  27.5 us (2%)
  local copies, waits for them, and re-layouts  15.6 us (1%)
  between operations  14.2 us (1%)
    all_gather x16, waiting for transfers between devices, from_root(): lax.all_gather(array, axis)  1060 us
    all_gather x1, waiting for transfers between devices, per_device(): right_block = lax.all_gather(upper_right, 'row', axis=0, tiled=True)  76.7 us
    all_gather x1, waiting for transfers between devices, per_device(): left_block = lax.all_gather(upper_left, 'col', axis=1, tiled=True)  57.5 us
  transfers between devices with their start and end apart: 18, of which 18 were waited for; matrix products, arithmetic and copies ran while one was open for 1% of the time, Pallas kernels for 0%

commit v1 on v0

v1 whole, which is shorter than its diff:
```python
import jax
import jax.numpy as jnp
from jax import lax
from jax.experimental import pallas as pl
from jax.experimental.pallas import tpu as pltpu
from jax.sharding import PartitionSpec as P

STEPS = 8
SIDE = 16
CHUNKS = 4
MESH = pl.DeviceIdType.MESH
BF16 = jnp.bfloat16
F32 = jnp.float32


def column_edges():
    edges = set()
    for chip in range(8):
        edges.add((2 * chip, 2 * chip + 1))
        if chip < 7:
            edges.add((2 * chip, 2 * chip + 2))
            edges.add((2 * chip + 1, 2 * chip + 2))
    edges |= {(0, far) for far in range(12, 16)}
    edges |= {(6, far) for far in range(8, 12)}
    edges |= {(2, 6), (0, 2)}
    edges |= {(far - 1, far) for far in range(9, 16)}
    return edges


def dot(left, right):
    return jnp.dot(left, right, preferred_element_type=F32)


def kernel(
    c_ref, a_ref, b_ref, u_ref, v_ref, al_ref, bl_ref, o_ref,
    ut, vt, inv, hbuf, ybuf, solved, xcol, xrow, abuf, bbuf,
    col_recv, row_recv, a_recv, b_recv,
    col_send, row_send, a_send, b_send, token,
):
    row = lax.axis_index("row")
    col = lax.axis_index("col")
    lag = SIDE - 1 - row
    x = row % 4
    y = row // 4
    even = col % 2 == 0
    size = c_ref.shape[0]
    part = size // CHUNKS
    parts = [pl.ds(p * part, part) for p in range(CHUNKS)]

    def row_of(x_to, y_to):
        return ((y_to + 4) % 4) * 4 + (x_to + 4) % 4

    x_minus, x_plus = row_of(x - 1, y), row_of(x + 1, y)
    y_minus, y_plus = row_of(x, y - 1), row_of(x, y + 1)

    def copy(src, dst, send, recv, to_row, to_col):
        return pltpu.make_async_remote_copy(
            src_ref=src, dst_ref=dst, send_sem=send, recv_sem=recv,
            device_id=(to_row, to_col), device_id_type=MESH,
        )

    def received(dst, recv):
        copy(dst, dst, recv, recv, row, col).wait_recv()

    barrier = pltpu.get_barrier_semaphore()
    for near in (x_minus, x_plus, y_minus, y_plus):
        pl.semaphore_signal(barrier, inc=1, device_id=(near, col), device_id_type=MESH)
    count = jnp.int32(4)
    edges = column_edges()
    for other in range(SIDE):
        near = sorted({b for a, b in edges if a == other} | {a for a, b in edges if b == other})
        hit = col == near[0]
        for mine in near[1:]:
            hit = hit | (col == mine)

        @pl.when(hit)
        def _():
            pl.semaphore_signal(barrier, inc=1, device_id=(row, other), device_id_type=MESH)

        count = count + hit.astype(jnp.int32)
    pl.semaphore_wait(barrier, count)

    def a_children(t):
        mine = lag > t
        last = STEPS - 1 - t
        onward = even & (t < 4) & (col + 2 <= last)
        back = (t >= 4) & ((col == 6) | (col == 2))
        side = even & (col + 1 <= last)
        return [
            (mine & (onward | back), row, jnp.where(onward, col + 2, jnp.where(col == 6, 2, 0))),
            (mine & side, row, jnp.minimum(col + 1, SIDE - 1)),
        ]

    def a_receives(t):
        return (lag > t) & ((col <= STEPS - 1 - t) | ((t >= 4) & ((col == 6) | (col == 2))))

    def b_children(k):
        xs = k % 4
        low = k < 4
        d = (xs - x + 4) % 4
        ring = low & (y == 3)
        start_low = low & (y == 0) & (x == xs)
        up = (start_low | (low & (y == 1) & (x == xs))) | (
            (~low) & ((y == 1) | (y == 2)) & (x == xs)
        )
        forward = (low & (y == 2) & (x >= xs) & (x < 3)) | (
            (~low) & (y == 3) & (x >= xs) & (x < 3)
        )
        mine = col > k
        return [
            (mine & start_low, y_minus, col),
            (mine & up, y_plus, col),
            (mine & ring & (d <= 1), x_minus, col),
            (mine & ((ring & (d == 0)) | forward), x_plus, col),
        ]

    def b_receives(k):
        xs = k % 4
        low = k < 4
        return (col > k) & (
            (low & ((y == 3) | ((y == 1) & (x == xs)) | ((y == 2) & (x >= xs))))
            | ((~low) & (((y == 2) & (x == xs)) | ((y == 3) & (x >= xs))))
        )

    def col_children(lk):
        rk = SIDE - 1 - lk
        xk, yk = rk % 4, rk // 4
        d = (xk - x + 4) % 4
        own = y == yk
        return [
            (own & (d <= 1), x_minus, col),
            (own & (d == 0), x_plus, col),
            ((own & (yk == 3)) | ((yk == 2) & ((y == 2) | (y == 1))), y_minus, col),
            ((yk == 3) & ((y == 3) | (y == 0)), y_plus, col),
        ]

    def row_children(k):
        return [
            (even & (col < SIDE - 1), row, jnp.minimum(col + 1, SIDE - 1)),
            ((col < SIDE - 2) & (even | (col == k)), row, jnp.minimum((col // 2 + 1) * 2, SIDE - 1)),
        ]

    def send_all(children, src, dst, sends, recv, where=True):
        for index, (condition, to_row, to_col) in enumerate(children):
            @pl.when(condition & where)
            def _():
                copy(src, dst, sends.at[index], recv, to_row, to_col).start()

    def sent_all(children, whole, sends, where=True):
        for index, (condition, to_row, to_col) in enumerate(children):
            @pl.when(condition & where)
            def _():
                copy(whole, whole, sends.at[index], sends.at[index], row, col).wait_send()

    is_b_source = (row < STEPS) & (col > row)
    b_own = jnp.minimum(row, STEPS - 1)
    send_all(b_children(b_own), b_ref, bbuf.at[b_own], b_send.at[b_own], b_recv.at[b_own], is_b_source)

    def a_source(t):
        mine = (col == SIDE - 1 - t) & (lag > t)
        first = (t == 0) | (t == 4)
        target = jnp.where(t < 4, 0, 6)
        this = copy(a_ref, abuf.at[t], a_send.at[t, 2], a_recv.at[t], row, target)

        @pl.when(mine & ~first)
        def _():
            pl.semaphore_wait(token, 1)

        @pl.when(mine)
        def _():
            this.start()
            this.wait_send()

        @pl.when(mine & (t != 3) & (t != 7) & (lag > t + 1))
        def _():
            pl.semaphore_signal(token, inc=1, device_id=(row, col - 1), device_id_type=MESH)

    a_source(jnp.int32(0))
    a_source(jnp.int32(4))

    ut[...] = u_ref[...].astype(F32).T.astype(BF16)
    vt[...] = v_ref[...].astype(F32).T.astype(BF16)
    sums = jnp.broadcast_to(al_ref[...], (size, size)).T + jnp.broadcast_to(bl_ref[...], (size, size))
    inv[...] = 1.0 / sums
    o_ref[...] = c_ref[...]

    def step(s, carry):
        a_in = a_receives(s)

        @pl.when(a_in)
        def _():
            received(abuf.at[s], a_recv.at[s])
            send_all(a_children(s), abuf.at[s], abuf.at[s], a_send.at[s], a_recv.at[s])

        @pl.when(s < 3)
        def _():
            a_source(s + 1)
            a_source(s + 5)

        @pl.when(b_receives(s))
        def _():
            received(bbuf.at[s], b_recv.at[s])
            send_all(b_children(s), bbuf.at[s], bbuf.at[s], b_send.at[s], b_recv.at[s])

        lk = s - col
        k = s - lag
        lk_at, k_at = jnp.maximum(lk, 0), jnp.maximum(k, 0)
        mine = lag + col == s
        from_col = (lk >= 0) & (lag != lk) & ((lk < 4) | (y < 3))
        from_row = (k >= 0) & (col > k)
        use_col = (lk >= 0) & (lag > lk)

        @pl.when(mine)
        def _():
            rounded = o_ref[...].astype(BF16)
            hbuf[...] = dot(ut[...], rounded).astype(BF16)
            ybuf[...] = (dot(hbuf[...], v_ref[...]) * inv[...]).astype(BF16)
            for rows in parts:
                turned = dot(u_ref[rows, :], ybuf[...]).astype(BF16)
                answer = dot(turned, vt[...])
                o_ref[rows, :] = answer
                solved[rows, :] = answer.astype(BF16)
                p = parts.index(rows)
                src = solved.at[rows]
                send_all(
                    col_children(lk_at), src, xcol.at[lk_at, rows], col_send.at[lk_at],
                    col_recv.at[lk_at, p],
                )
                send_all(
                    row_children(k_at), src, xrow.at[k_at, rows], row_send.at[k_at],
                    row_recv.at[k_at, p],
                )

        for p, rows in enumerate(parts):
            @pl.when(from_col)
            def _():
                tile = xcol.at[lk_at, rows]
                received(tile, col_recv.at[lk_at, p])
                send_all(col_children(lk_at), tile, tile, col_send.at[lk_at], col_recv.at[lk_at, p])

            @pl.when(from_row)
            def _():
                tile = xrow.at[k_at, rows]
                received(tile, row_recv.at[k_at, p])
                send_all(row_children(k_at), tile, tile, row_send.at[k_at], row_recv.at[k_at, p])

            @pl.when(use_col)
            def _():
                o_ref[...] -= dot(abuf[lk_at, :, rows], xcol[lk_at, rows, :])

            @pl.when(from_row)
            def _():
                o_ref[rows, :] -= dot(xrow[k_at, rows, :], bbuf[k_at])

        return carry

    lax.fori_loop(0, STEPS, step, 0)

    send_b = is_b_source
    sent_all(b_children(b_own), bbuf.at[b_own], b_send.at[b_own], send_b)

    def drain(s, carry):
        sent_all(a_children(s), abuf.at[s], a_send.at[s], a_receives(s))
        sent_all(b_children(s), bbuf.at[s], b_send.at[s], b_receives(s))
        lk = s - col
        k = s - lag
        lk_at, k_at = jnp.maximum(lk, 0), jnp.maximum(k, 0)
        source = lag + col == s
        from_col = (lk >= 0) & ((lk < 4) | (y < 3))
        from_row = (k >= 0) & (col >= k)
        sent_all(col_children(lk_at), xcol.at[lk_at], col_send.at[lk_at], from_col)
        sent_all(row_children(k_at), xrow.at[k_at], row_send.at[k_at], from_row)
        return carry

    lax.fori_loop(0, STEPS, drain, 0)


def per_device(right_side, upper_left, upper_right, vectors_left, vectors_right, values_left, values_right):
    size = right_side.shape[0]
    tile = pltpu.VMEM((size, size), BF16)
    tiles = pltpu.VMEM((STEPS, size, size), BF16)
    sems = pltpu.SemaphoreType.DMA
    vmem = pl.BlockSpec(memory_space=pltpu.VMEM)
    return pl.pallas_call(
        kernel,
        out_shape=jax.ShapeDtypeStruct((size, size), F32),
        in_specs=[vmem] * 7,
        out_specs=vmem,
        scratch_shapes=[
            tile, tile, pltpu.VMEM((size, size), F32), tile, tile, tile,
            tiles, tiles, tiles, tiles,
            sems((STEPS, CHUNKS)), sems((STEPS, CHUNKS)), sems((STEPS,)), sems((STEPS,)),
            sems((STEPS, 4)), sems((STEPS, 2)), sems((STEPS, 3)), sems((STEPS, 4)),
            pltpu.SemaphoreType.REGULAR,
        ],
        compiler_params=pltpu.CompilerParams(
            collective_id=0, has_side_effects=True, vmem_limit_bytes=48 << 20
        ),
        name="sylvester",
    )(
        right_side, upper_left, upper_right, vectors_left, vectors_right,
        values_left.reshape(1, size), values_right.reshape(1, size),
    )


def solution(mesh):
    in_specs = (
        P("row", "col"),
        P("row", "col"),
        P("row", "col"),
        P("row", None),
        P("col", None),
        P("row"),
        P("col"),
    )
    return jax.shard_map(
        per_device, mesh=mesh, in_specs=in_specs, out_specs=P("row", "col"), check_vma=False
    )
```

time: 1260 us -> 218 us (0.17)
  waiting for transfers between devices: 1200 us -> 0 us
  Pallas kernels: 0 us -> 210 us
  matrix products: 27.5 us -> 0 us
  between operations: 14.2 us -> 0.02 us
    all_gather x18 -> x0, waiting for transfers between devices: 1190 us -> none  [the longest x16 1060 us: from_root(): lax.all_gather(array, axis)]
    pallas_call x0 -> x1, Pallas kernels: none -> 210 us  [per_device(): pl.pallas_call(kernel, out_shape=jax.ShapeDtypeStruct((size, size), F32),...]
    dot_general x16 -> x0, matrix products: 27.5 us -> none  [the longest x8 14.1 us: per_device(): jnp.dot(from_left, right_tile, preferred_element_type=jnp.float32)]
  transfers between devices with their start and end apart: 18 -> 0, of which waited for: 18 -> 0; matrix products, arithmetic and copies ran while one was open for 1% -> 0% of each run, Pallas kernels for 0% -> 0%
where the time goes in v1:
time: 218 us; the launch traced here: 217 us
  Pallas kernels  210 us (96%)
  local copies, waits for them, and re-layouts  7.72 us (4%)
    pallas_call x1, Pallas kernels, per_device(): pl.pallas_call(kernel, out_shape=jax.ShapeDtypeStruct((size, size), F32),...  210 us
    unnamed x15, local copies, waits for them, and re-layouts  7.72 us

profile of v1, /device:TPU:2, one launch (start us, length us, event | category | flops | bytes accessed | tf_op | source)
XLA Modules:
  0.0 217.5 jit_solution(12167141062439187664)
XLA Ops:
  0.0 0.0 copy-start.5
  0.0 0.7 copy-done.5
  0.7 0.0 copy-start
  0.7 1.2 copy-done
  1.9 0.0 copy-start.1
  1.9 1.0 copy-done.1
  3.0 0.0 copy-start.2
  3.0 1.0 copy-done.2
  4.0 0.0 copy-start.3
  4.0 1.0 copy-done.3
  5.0 0.0 copy-start.4
  5.0 1.0 copy-done.4
  6.1 0.0 copy-start.6
  6.1 0.7 copy-done.6
  6.8 209.7 %sylvester.1 = f32[512,512]{1,0:T(8,128)S(1)} custom-call(f32[512,512]{1,0:T(8,128)S(1)} %copy-done, bf16[512,512]{1,0:T(8,128)(2,1)S(1)} %copy-done.1, bf16[512,512]{1,0:T(8,128)(2,1)S(1)} %copy-done.2, bf16[512,512]{1,0:T(8,128)(2,1)S(1)} %copy-done.3, bf16[512,512]{1,0:T(8,128)(2,1)S(1)} %copy-done.4, f32[1,512]{1,0:T(1,128)S(1)} %bitcast.2, ...), custom_call_target="tpu_custom_call" | custom-call | tf_op jit(solution)/shard_map/sylvester/pallas_call | solution.py:284
  216.5 1.0 copy.9
Async XLA Ops:
  0.0 0.7 copy-start.5
  0.7 1.2 copy-start
  1.9 1.0 copy-start.1
  3.0 1.0 copy-start.2
  4.0 1.0 copy-start.3
  5.0 1.0 copy-start.4
  6.1 0.7 copy-start.6

commit v2 on v1

--- a/solution.py
+++ b/solution.py
@@ -32,10 +32,11 @@
 
 
 def kernel(
-    c_ref, a_ref, b_ref, u_ref, v_ref, al_ref, bl_ref, o_ref,
+    c_any, a_any, b_any, u_any, v_any, al_any, bl_any, o_ref,
+    u_ref, v_ref, al_ref, bl_ref,
     ut, vt, inv, hbuf, ybuf, solved, xcol, xrow, abuf, bbuf,
     col_recv, row_recv, a_recv, b_recv,
-    col_send, row_send, a_send, b_send, token,
+    col_send, row_send, a_send, b_send, a_first, loaded, token,
 ):
     row = lax.axis_index("row")
     col = lax.axis_index("col")
@@ -43,7 +44,7 @@
     x = row % 4
     y = row // 4
     even = col % 2 == 0
-    size = c_ref.shape[0]
+    size = o_ref.shape[0]
     part = size // CHUNKS
     parts = [pl.ds(p * part, part) for p in range(CHUNKS)]
 
@@ -61,6 +62,15 @@
 
     def received(dst, recv):
         copy(dst, dst, recv, recv, row, col).wait_recv()
+
+    loads = [
+        pltpu.make_async_copy(src, dst, loaded.at[index])
+        for index, (src, dst) in enumerate(
+            [(c_any, o_ref), (u_any, u_ref), (v_any, v_ref), (al_any, al_ref), (bl_any, bl_ref)]
+        )
+    ]
+    for load in loads:
+        load.start()
 
     barrier = pltpu.get_barrier_semaphore()
     for near in (x_minus, x_plus, y_minus, y_plus):
@@ -154,53 +164,58 @@
 
     is_b_source = (row < STEPS) & (col > row)
     b_own = jnp.minimum(row, STEPS - 1)
-    send_all(b_children(b_own), b_ref, bbuf.at[b_own], b_send.at[b_own], b_recv.at[b_own], is_b_source)
-
-    def a_source(t):
-        mine = (col == SIDE - 1 - t) & (lag > t)
-        first = (t == 0) | (t == 4)
-        target = jnp.where(t < 4, 0, 6)
-        this = copy(a_ref, abuf.at[t], a_send.at[t, 2], a_recv.at[t], row, target)
-
-        @pl.when(mine & ~first)
-        def _():
-            pl.semaphore_wait(token, 1)
-
-        @pl.when(mine)
-        def _():
+    for p, rows in enumerate(parts):
+        send_all(
+            b_children(b_own), b_any.at[rows], bbuf.at[b_own, rows], b_send.at[b_own],
+            b_recv.at[b_own, p], is_b_source,
+        )
+
+    t_own = jnp.minimum(SIDE - 1 - col, STEPS - 1)
+    is_a_source = (col >= SIDE - STEPS) & (lag > t_own)
+    a_target = jnp.where(t_own < 4, 0, 6)
+    a_copies = [
+        copy(
+            a_any.at[rows], abuf.at[t_own, rows], a_first.at[p], a_recv.at[t_own, p], row, a_target
+        )
+        for p, rows in enumerate(parts)
+    ]
+
+    @pl.when(is_a_source & (t_own != 0) & (t_own != 4))
+    def _():
+        pl.semaphore_wait(token, 1)
+
+    @pl.when(is_a_source)
+    def _():
+        for this in a_copies:
             this.start()
+        for this in a_copies[:-1]:
             this.wait_send()
 
-        @pl.when(mine & (t != 3) & (t != 7) & (lag > t + 1))
-        def _():
-            pl.semaphore_signal(token, inc=1, device_id=(row, col - 1), device_id_type=MESH)
-
-    a_source(jnp.int32(0))
-    a_source(jnp.int32(4))
-
+    @pl.when(is_a_source & (t_own != 3) & (t_own != 7) & (lag > t_own + 1))
+    def _():
+        pl.semaphore_signal(token, inc=1, device_id=(row, col - 1), device_id_type=MESH)
+
+    for load in loads:
+        load.wait()
     ut[...] = u_ref[...].astype(F32).T.astype(BF16)
     vt[...] = v_ref[...].astype(F32).T.astype(BF16)
     sums = jnp.broadcast_to(al_ref[...], (size, size)).T + jnp.broadcast_to(bl_ref[...], (size, size))
     inv[...] = 1.0 / sums
-    o_ref[...] = c_ref[...]
 
     def step(s, carry):
-        a_in = a_receives(s)
-
-        @pl.when(a_in)
-        def _():
-            received(abuf.at[s], a_recv.at[s])
-            send_all(a_children(s), abuf.at[s], abuf.at[s], a_send.at[s], a_recv.at[s])
-
-        @pl.when(s < 3)
-        def _():
-            a_source(s + 1)
-            a_source(s + 5)
-
-        @pl.when(b_receives(s))
-        def _():
-            received(bbuf.at[s], b_recv.at[s])
-            send_all(b_children(s), bbuf.at[s], bbuf.at[s], b_send.at[s], b_recv.at[s])
+        for p, rows in enumerate(parts):
+            @pl.when(a_receives(s))
+            def _():
+                tile = abuf.at[s, rows]
+                received(tile, a_recv.at[s, p])
+                send_all(a_children(s), tile, tile, a_send.at[s], a_recv.at[s, p])
+
+        for p, rows in enumerate(parts):
+            @pl.when(b_receives(s))
+            def _():
+                tile = bbuf.at[s, rows]
+                received(tile, b_recv.at[s, p])
+                send_all(b_children(s), tile, tile, b_send.at[s], b_recv.at[s, p])
 
         lk = s - col
         k = s - lag
@@ -256,8 +271,11 @@
 
     lax.fori_loop(0, STEPS, step, 0)
 
-    send_b = is_b_source
-    sent_all(b_children(b_own), bbuf.at[b_own], b_send.at[b_own], send_b)
+    sent_all(b_children(b_own), bbuf.at[b_own], b_send.at[b_own], is_b_source)
+
+    @pl.when(is_a_source)
+    def _():
+        a_copies[-1].wait_send()
 
     def drain(s, carry):
         sent_all(a_children(s), abuf.at[s], a_send.at[s], a_receives(s))
@@ -284,13 +302,15 @@
     return pl.pallas_call(
         kernel,
         out_shape=jax.ShapeDtypeStruct((size, size), F32),
-        in_specs=[vmem] * 7,
+        in_specs=[pl.BlockSpec(memory_space=pl.ANY)] * 7,
         out_specs=vmem,
         scratch_shapes=[
+            tile, tile, pltpu.VMEM((1, size), F32), pltpu.VMEM((1, size), F32),
             tile, tile, pltpu.VMEM((size, size), F32), tile, tile, tile,
             tiles, tiles, tiles, tiles,
-            sems((STEPS, CHUNKS)), sems((STEPS, CHUNKS)), sems((STEPS,)), sems((STEPS,)),
-            sems((STEPS, 4)), sems((STEPS, 2)), sems((STEPS, 3)), sems((STEPS, 4)),
+            sems((STEPS, CHUNKS)), sems((STEPS, CHUNKS)), sems((STEPS, CHUNKS)), sems((STEPS, CHUNKS)),
+            sems((STEPS, 4)), sems((STEPS, 2)), sems((STEPS, 2)), sems((STEPS, 4)),
+            sems((CHUNKS,)), sems((5,)),
             pltpu.SemaphoreType.REGULAR,
         ],
         compiler_params=pltpu.CompilerParams(

time: 218 us -> 185 us (0.85)
  Pallas kernels: 210 us -> 175 us
    pallas_call x1, Pallas kernels: 210 us -> 175 us  [per_device(): pl.pallas_call(kernel, out_shape=jax.ShapeDtypeStruct((size, size), F32),...]
where the time goes in v2:
time: 185 us; the launch traced here: 183 us
  Pallas kernels  175 us (95%)
  local copies, waits for them, and re-layouts  7.72 us (4%)
    pallas_call x1, Pallas kernels, per_device(): pl.pallas_call(kernel, out_shape=jax.ShapeDtypeStruct((size, size), F32),...  175 us
    unnamed x15, local copies, waits for them, and re-layouts  7.72 us

profile of v2, /device:TPU:2, one launch (start us, length us, event | category | flops | bytes accessed | tf_op | source)
XLA Modules:
  0.0 182.9 jit_solution(3621682160319463236)
XLA Ops:
  0.0 0.0 copy-start.5
  0.0 0.7 copy-done.5
  0.7 0.0 copy-start
  0.7 1.2 copy-done
  1.9 0.0 copy-start.1
  1.9 1.0 copy-done.1
  3.0 0.0 copy-start.2
  3.0 1.0 copy-done.2
  4.0 0.0 copy-start.3
  4.0 1.0 copy-done.3
  5.0 0.0 copy-start.4
  5.0 1.0 copy-done.4
  6.1 0.0 copy-start.6
  6.1 0.7 copy-done.6
  6.8 175.2 %sylvester.1 = f32[512,512]{1,0:T(8,128)S(1)} custom-call(f32[512,512]{1,0:T(8,128)S(1)} %copy-done, bf16[512,512]{1,0:T(8,128)(2,1)S(1)} %copy-done.1, bf16[512,512]{1,0:T(8,128)(2,1)S(1)} %copy-done.2, bf16[512,512]{1,0:T(8,128)(2,1)S(1)} %copy-done.3, bf16[512,512]{1,0:T(8,128)(2,1)S(1)} %copy-done.4, f32[1,512]{1,0:T(1,128)S(1)} %bitcast.2, ...), custom_call_target="tpu_custom_call" | custom-call | tf_op jit(solution)/shard_map/sylvester/pallas_call | solution.py:302
  182.0 1.0 copy.9
Async XLA Ops:
  0.0 0.7 copy-start.5
  0.7 1.2 copy-start
  1.9 1.0 copy-start.1
  3.0 1.0 copy-start.2
  4.0 1.0 copy-start.3
  5.0 1.0 copy-start.4
  6.1 0.7 copy-start.6

commit v3 on v2

--- a/solution.py
+++ b/solution.py
@@ -21,8 +21,8 @@
             edges.add((2 * chip, 2 * chip + 2))
             edges.add((2 * chip + 1, 2 * chip + 2))
     edges |= {(0, far) for far in range(12, 16)}
-    edges |= {(6, far) for far in range(8, 12)}
-    edges |= {(2, 6), (0, 2)}
+    edges |= {(2, far) for far in range(8, 12)}
+    edges |= {(0, 2)}
     edges |= {(far - 1, far) for far in range(9, 16)}
     return edges
 
@@ -75,7 +75,11 @@
     barrier = pltpu.get_barrier_semaphore()
     for near in (x_minus, x_plus, y_minus, y_plus):
         pl.semaphore_signal(barrier, inc=1, device_id=(near, col), device_id_type=MESH)
-    count = jnp.int32(4)
+    for mine, other in ((12, 11), (11, 12)):
+        @pl.when(row == mine)
+        def _():
+            pl.semaphore_signal(barrier, inc=1, device_id=(other, col), device_id_type=MESH)
+    count = 4 + ((row == 11) | (row == 12)).astype(jnp.int32)
     edges = column_edges()
     for other in range(SIDE):
         near = sorted({b for a, b in edges if a == other} | {a for a, b in edges if b == other})
@@ -94,42 +98,44 @@
         mine = lag > t
         last = STEPS - 1 - t
         onward = even & (t < 4) & (col + 2 <= last)
-        back = (t >= 4) & ((col == 6) | (col == 2))
+        back = (t >= 4) & (col == 2)
         side = even & (col + 1 <= last)
         return [
-            (mine & (onward | back), row, jnp.where(onward, col + 2, jnp.where(col == 6, 2, 0))),
+            (mine & (onward | back), row, jnp.where(onward, col + 2, 0)),
             (mine & side, row, jnp.minimum(col + 1, SIDE - 1)),
         ]
 
     def a_receives(t):
-        return (lag > t) & ((col <= STEPS - 1 - t) | ((t >= 4) & ((col == 6) | (col == 2))))
+        return (lag > t) & ((col <= STEPS - 1 - t) | ((t >= 4) & (col == 2)))
 
     def b_children(k):
         xs = k % 4
         low = k < 4
+        high = ~low
+        right = x >= xs
         d = (xs - x + 4) % 4
-        ring = low & (y == 3)
-        start_low = low & (y == 0) & (x == xs)
-        up = (start_low | (low & (y == 1) & (x == xs))) | (
-            (~low) & ((y == 1) | (y == 2)) & (x == xs)
-        )
-        forward = (low & (y == 2) & (x >= xs) & (x < 3)) | (
-            (~low) & (y == 3) & (x >= xs) & (x < 3)
-        )
+        up, down = high & (k % 2 == 0), high & (k % 2 == 1)
         mine = col > k
         return [
-            (mine & start_low, y_minus, col),
-            (mine & up, y_plus, col),
-            (mine & ring & (d <= 1), x_minus, col),
-            (mine & ((ring & (d == 0)) | forward), x_plus, col),
+            (mine & ((low & (y == 0)) | (down & right & ((y == 1) | (y == 0)))), y_minus, col),
+            (
+                mine & right & ((low & ((y == 0) | (y == 1))) | (up & ((y == 1) | (y == 2)))),
+                y_plus, col,
+            ),
+            (mine & low & (y == 0) & (d == 0), x_minus, col),
+            (
+                mine & ((low & (y == 0) & ((d == 0) | (d == 3))) | (high & (y == 1) & right & (x < 3))),
+                x_plus, col,
+            ),
         ]
 
     def b_receives(k):
-        xs = k % 4
+        right = x >= k % 4
         low = k < 4
-        return (col > k) & (
-            (low & ((y == 3) | ((y == 1) & (x == xs)) | ((y == 2) & (x >= xs))))
-            | ((~low) & (((y == 2) & (x == xs)) | ((y == 3) & (x >= xs))))
+        across = jnp.where(k % 2 == 0, 2, 0)
+        return (col > k) & (row != k) & (
+            (low & ((y == 3) | (y == 0) | right))
+            | ((~low) & right & ((y == 1) | (y == 3) | (y == across)))
         )
 
     def col_children(lk):
@@ -138,9 +144,13 @@
         d = (xk - x + 4) % 4
         own = y == yk
         return [
-            (own & (d <= 1), x_minus, col),
-            (own & (d == 0), x_plus, col),
-            ((own & (yk == 3)) | ((yk == 2) & ((y == 2) | (y == 1))), y_minus, col),
+            (own & (d == 0), x_minus, col),
+            (own & (d == 0) & (lk == 3), row_of(3, 2), col),
+            (own & ((d == 0) | (d == 3)), x_plus, col),
+            (
+                (own & (yk == 3) & ((lk != 3) | (x != 3))) | ((yk == 2) & ((y == 2) | (y == 1))),
+                y_minus, col,
+            ),
             ((yk == 3) & ((y == 3) | (y == 0)), y_plus, col),
         ]
 
@@ -172,7 +182,7 @@
 
     t_own = jnp.minimum(SIDE - 1 - col, STEPS - 1)
     is_a_source = (col >= SIDE - STEPS) & (lag > t_own)
-    a_target = jnp.where(t_own < 4, 0, 6)
+    a_target = jnp.where(t_own < 4, 0, 2)
     a_copies = [
         copy(
             a_any.at[rows], abuf.at[t_own, rows], a_first.at[p], a_recv.at[t_own, p], row, a_target
@@ -202,20 +212,28 @@
     sums = jnp.broadcast_to(al_ref[...], (size, size)).T + jnp.broadcast_to(bl_ref[...], (size, size))
     inv[...] = 1.0 / sums
 
+    def take_b(k, carry):
+        for p, rows in enumerate(parts):
+            @pl.when(b_receives(k) & ((y < 2) | ((y == 2) & (k > 3))))
+            def _():
+                tile = bbuf.at[k, rows]
+                received(tile, b_recv.at[k, p])
+                send_all(b_children(k), tile, tile, b_send.at[k], b_recv.at[k, p])
+
+        return carry
+
+    lax.fori_loop(0, STEPS, take_b, 0)
+
     def step(s, carry):
-        for p, rows in enumerate(parts):
-            @pl.when(a_receives(s))
-            def _():
-                tile = abuf.at[s, rows]
-                received(tile, a_recv.at[s, p])
-                send_all(a_children(s), tile, tile, a_send.at[s], a_recv.at[s, p])
-
-        for p, rows in enumerate(parts):
-            @pl.when(b_receives(s))
-            def _():
-                tile = bbuf.at[s, rows]
-                received(tile, b_recv.at[s, p])
-                send_all(b_children(s), tile, tile, b_send.at[s], b_recv.at[s, p])
+        first = jnp.where(s == 0, 0, jnp.where(s < 3, s + 1, jnp.minimum(s + 3, STEPS - 1)))
+        second = jnp.where(s == 0, 1, jnp.minimum(s + 3, STEPS - 1))
+        for t, here in ((first, s < 5), (second, s < 3)):
+            for p, rows in enumerate(parts):
+                @pl.when(here & even & a_receives(t))
+                def _():
+                    tile = abuf.at[t, rows]
+                    received(tile, a_recv.at[t, p])
+                    send_all(a_children(t), tile, tile, a_send.at[t], a_recv.at[t, p])
 
         lk = s - col
         k = s - lag
@@ -247,25 +265,35 @@
                 )
 
         for p, rows in enumerate(parts):
+            @pl.when(from_row)
+            def _():
+                tile = xrow.at[k_at, rows]
+                received(tile, row_recv.at[k_at, p])
+                send_all(row_children(k_at), tile, tile, row_send.at[k_at], row_recv.at[k_at, p])
+
+        for p, rows in enumerate(parts):
+            @pl.when(from_row)
+            def _():
+                received(bbuf.at[k_at, rows], b_recv.at[k_at, p])
+
+            @pl.when(use_col & ~even)
+            def _():
+                received(abuf.at[lk_at, rows], a_recv.at[lk_at, p])
+
+        for p, rows in enumerate(parts):
+            @pl.when(from_row)
+            def _():
+                o_ref[rows, :] -= dot(xrow[k_at, rows, :], bbuf[k_at])
+
             @pl.when(from_col)
             def _():
                 tile = xcol.at[lk_at, rows]
                 received(tile, col_recv.at[lk_at, p])
                 send_all(col_children(lk_at), tile, tile, col_send.at[lk_at], col_recv.at[lk_at, p])
 
-            @pl.when(from_row)
-            def _():
-                tile = xrow.at[k_at, rows]
-                received(tile, row_recv.at[k_at, p])
-                send_all(row_children(k_at), tile, tile, row_send.at[k_at], row_recv.at[k_at, p])
-
             @pl.when(use_col)
             def _():
                 o_ref[...] -= dot(abuf[lk_at, :, rows], xcol[lk_at, rows, :])
-
-            @pl.when(from_row)
-            def _():
-                o_ref[rows, :] -= dot(xrow[k_at, rows, :], bbuf[k_at])
 
         return carry
 
@@ -309,7 +337,7 @@
             tile, tile, pltpu.VMEM((size, size), F32), tile, tile, tile,
             tiles, tiles, tiles, tiles,
             sems((STEPS, CHUNKS)), sems((STEPS, CHUNKS)), sems((STEPS, CHUNKS)), sems((STEPS, CHUNKS)),
-            sems((STEPS, 4)), sems((STEPS, 2)), sems((STEPS, 2)), sems((STEPS, 4)),
+            sems((STEPS, 5)), sems((STEPS, 2)), sems((STEPS, 2)), sems((STEPS, 4)),
             sems((CHUNKS,)), sems((5,)),
             pltpu.SemaphoreType.REGULAR,
         ],

time: 185 us -> 152 us (0.82)
  the two profiles are of different devices: /device:TPU:2 before, /device:TPU:243 now
where the time goes in v3:
time: 152 us; the launch traced here: 151 us
  Pallas kernels  144 us (95%)
  local copies, waits for them, and re-layouts  7.72 us (5%)
    pallas_call x1, Pallas kernels, per_device(): pl.pallas_call(kernel, out_shape=jax.ShapeDtypeStruct((size, size), F32),...  144 us
    unnamed x15, local copies, waits for them, and re-layouts  7.72 us

profile of v3, /device:TPU:243, one launch (start us, length us, event | category | flops | bytes accessed | tf_op | source)
XLA Modules:
  0.0 151.5 jit_solution(11285067666993690062)
XLA Ops:
  0.0 0.0 copy-start.5
  0.0 0.7 copy-done.5
  0.7 0.0 copy-start
  0.7 1.2 copy-done
  1.9 0.0 copy-start.1
  1.9 1.0 copy-done.1
  3.0 0.0 copy-start.2
  3.0 1.0 copy-done.2
  4.0 0.0 copy-start.3
  4.0 1.0 copy-done.3
  5.0 0.0 copy-start.4
  5.0 1.0 copy-done.4
  6.1 0.0 copy-start.6
  6.1 0.7 copy-done.6
  6.8 143.7 %sylvester.1 = f32[512,512]{1,0:T(8,128)S(1)} custom-call(f32[512,512]{1,0:T(8,128)S(1)} %copy-done, bf16[512,512]{1,0:T(8,128)(2,1)S(1)} %copy-done.1, bf16[512,512]{1,0:T(8,128)(2,1)S(1)} %copy-done.2, bf16[512,512]{1,0:T(8,128)(2,1)S(1)} %copy-done.3, bf16[512,512]{1,0:T(8,128)(2,1)S(1)} %copy-done.4, f32[1,512]{1,0:T(1,128)S(1)} %bitcast.2, ...), custom_call_target="tpu_custom_call" | custom-call | tf_op jit(solution)/shard_map/sylvester/pallas_call | solution.py:330
  150.5 1.0 copy.9
Async XLA Ops:
  0.0 0.7 copy-start.5
  0.7 1.2 copy-start
  1.9 1.0 copy-start.1
  3.0 1.0 copy-start.2
  4.0 1.0 copy-start.3
  5.0 1.0 copy-start.4
  6.1 0.7 copy-start.6

commit v4 on v3

--- a/solution.py
+++ b/solution.py
@@ -20,8 +20,8 @@
         if chip < 7:
             edges.add((2 * chip, 2 * chip + 2))
             edges.add((2 * chip + 1, 2 * chip + 2))
-    edges |= {(0, far) for far in range(12, 16)}
-    edges |= {(2, far) for far in range(8, 12)}
+    edges |= {(0, far) for far in range(10, 16)}
+    edges |= {(2, far) for far in range(8, 10)}
     edges |= {(0, 2)}
     edges |= {(far - 1, far) for far in range(9, 16)}
     return edges
@@ -97,8 +97,8 @@
     def a_children(t):
         mine = lag > t
         last = STEPS - 1 - t
-        onward = even & (t < 4) & (col + 2 <= last)
-        back = (t >= 4) & (col == 2)
+        onward = even & (t < 6) & (col + 2 <= last)
+        back = (t >= 6) & (col == 2)
         side = even & (col + 1 <= last)
         return [
             (mine & (onward | back), row, jnp.where(onward, col + 2, 0)),
@@ -106,7 +106,7 @@
         ]
 
     def a_receives(t):
-        return (lag > t) & ((col <= STEPS - 1 - t) | ((t >= 4) & (col == 2)))
+        return (lag > t) & ((col <= STEPS - 1 - t) | ((t >= 6) & (col == 2)))
 
     def b_children(k):
         xs = k % 4
@@ -182,7 +182,7 @@
 
     t_own = jnp.minimum(SIDE - 1 - col, STEPS - 1)
     is_a_source = (col >= SIDE - STEPS) & (lag > t_own)
-    a_target = jnp.where(t_own < 4, 0, 2)
+    a_target = jnp.where(t_own < 6, 0, 2)
     a_copies = [
         copy(
             a_any.at[rows], abuf.at[t_own, rows], a_first.at[p], a_recv.at[t_own, p], row, a_target
@@ -190,7 +190,7 @@
         for p, rows in enumerate(parts)
     ]
 
-    @pl.when(is_a_source & (t_own != 0) & (t_own != 4))
+    @pl.when(is_a_source & (t_own != 0) & (t_own != 6))
     def _():
         pl.semaphore_wait(token, 1)
 
@@ -201,7 +201,7 @@
         for this in a_copies[:-1]:
             this.wait_send()
 
-    @pl.when(is_a_source & (t_own != 3) & (t_own != 7) & (lag > t_own + 1))
+    @pl.when(is_a_source & (t_own != 5) & (t_own != 7) & (lag > t_own + 1))
     def _():
         pl.semaphore_signal(token, inc=1, device_id=(row, col - 1), device_id_type=MESH)
 
@@ -212,28 +212,41 @@
     sums = jnp.broadcast_to(al_ref[...], (size, size)).T + jnp.broadcast_to(bl_ref[...], (size, size))
     inv[...] = 1.0 / sums
 
-    def take_b(k, carry):
-        for p, rows in enumerate(parts):
-            @pl.when(b_receives(k) & ((y < 2) | ((y == 2) & (k > 3))))
-            def _():
-                tile = bbuf.at[k, rows]
-                received(tile, b_recv.at[k, p])
-                send_all(b_children(k), tile, tile, b_send.at[k], b_recv.at[k, p])
-
+    def relay(condition, children, buffer, recvs, sends):
+        @pl.when(condition)
+        def _():
+            for p, rows in enumerate(parts):
+                tile = buffer.at[rows]
+                received(tile, recvs.at[p])
+                send_all(children, tile, tile, sends, recvs.at[p])
+
+    def take_b(q, carry):
+        near = jnp.where(q % 3 == 0, 1, jnp.where(q % 3 == 1, 3, 2))
+        source_row = jnp.where(q < 3, (x + near) % 4, jnp.where(q == 3, 5, 7))
+        high = x + 3 - q
+        turn = jnp.where(q == 3, 0, jnp.where(q == 4, 1, jnp.where(q == 5, 3, 2)))
+        k = jnp.where(
+            y == 0, source_row,
+            jnp.where(y == 1, jnp.where(q < 3, high, (x + turn) % 4), 4 + 2 * q),
+        )
+        valid = jnp.where(
+            y == 0, q < 5, jnp.where(y == 1, ((q >= 3) | (high >= 4)) & (q < 7), (y == 2) & (q < 2))
+        )
+        at = jnp.clip(k, 0, STEPS - 1)
+        relay(valid & b_receives(at), b_children(at), bbuf.at[at], b_recv.at[at], b_send.at[at])
         return carry
 
-    lax.fori_loop(0, STEPS, take_b, 0)
+    @pl.when((y < 3) & (col > 0))
+    def _():
+        lax.fori_loop(0, STEPS - 1, take_b, 0)
 
     def step(s, carry):
-        first = jnp.where(s == 0, 0, jnp.where(s < 3, s + 1, jnp.minimum(s + 3, STEPS - 1)))
-        second = jnp.where(s == 0, 1, jnp.minimum(s + 3, STEPS - 1))
-        for t, here in ((first, s < 5), (second, s < 3)):
-            for p, rows in enumerate(parts):
-                @pl.when(here & even & a_receives(t))
-                def _():
-                    tile = abuf.at[t, rows]
-                    received(tile, a_recv.at[t, p])
-                    send_all(a_children(t), tile, tile, a_send.at[t], a_recv.at[t, p])
+        @pl.when(even & (col < STEPS) & (s < 4))
+        def _():
+            first = jnp.where(s < 2, 2 * s, jnp.where(s == 2, 4, 5))
+            second = jnp.minimum(jnp.where(s < 2, 2 * s + 1, s + 4), STEPS - 1)
+            for t in (first, second):
+                relay(a_receives(t), a_children(t), abuf.at[t], a_recv.at[t], a_send.at[t])
 
         lk = s - col
         k = s - lag
@@ -243,57 +256,50 @@
         from_row = (k >= 0) & (col > k)
         use_col = (lk >= 0) & (lag > lk)
 
+        to_col, to_row = col_children(lk_at), row_children(k_at)
+
         @pl.when(mine)
         def _():
             rounded = o_ref[...].astype(BF16)
             hbuf[...] = dot(ut[...], rounded).astype(BF16)
             ybuf[...] = (dot(hbuf[...], v_ref[...]) * inv[...]).astype(BF16)
-            for rows in parts:
+            for p, rows in enumerate(parts):
                 turned = dot(u_ref[rows, :], ybuf[...]).astype(BF16)
                 answer = dot(turned, vt[...])
                 o_ref[rows, :] = answer
                 solved[rows, :] = answer.astype(BF16)
-                p = parts.index(rows)
                 src = solved.at[rows]
                 send_all(
-                    col_children(lk_at), src, xcol.at[lk_at, rows], col_send.at[lk_at],
-                    col_recv.at[lk_at, p],
+                    to_col, src, xcol.at[lk_at, rows], col_send.at[lk_at], col_recv.at[lk_at, p]
                 )
                 send_all(
-                    row_children(k_at), src, xrow.at[k_at, rows], row_send.at[k_at],
-                    row_recv.at[k_at, p],
+                    to_row, src, xrow.at[k_at, rows], row_send.at[k_at], row_recv.at[k_at, p]
                 )
 
-        for p, rows in enumerate(parts):
-            @pl.when(from_row)
-            def _():
-                tile = xrow.at[k_at, rows]
-                received(tile, row_recv.at[k_at, p])
-                send_all(row_children(k_at), tile, tile, row_send.at[k_at], row_recv.at[k_at, p])
-
-        for p, rows in enumerate(parts):
-            @pl.when(from_row)
-            def _():
+        relay(from_row, to_row, xrow.at[k_at], row_recv.at[k_at], row_send.at[k_at])
+
+        @pl.when(from_row)
+        def _():
+            for p, rows in enumerate(parts):
                 received(bbuf.at[k_at, rows], b_recv.at[k_at, p])
-
-            @pl.when(use_col & ~even)
-            def _():
+            for p, rows in enumerate(parts):
+                o_ref[rows, :] -= dot(xrow[k_at, rows, :], bbuf[k_at])
+
+        @pl.when(use_col & ~even)
+        def _():
+            for p, rows in enumerate(parts):
                 received(abuf.at[lk_at, rows], a_recv.at[lk_at, p])
 
-        for p, rows in enumerate(parts):
-            @pl.when(from_row)
-            def _():
-                o_ref[rows, :] -= dot(xrow[k_at, rows, :], bbuf[k_at])
-
-            @pl.when(from_col)
-            def _():
+        @pl.when(from_col)
+        def _():
+            for p, rows in enumerate(parts):
                 tile = xcol.at[lk_at, rows]
                 received(tile, col_recv.at[lk_at, p])
-                send_all(col_children(lk_at), tile, tile, col_send.at[lk_at], col_recv.at[lk_at, p])
-
-            @pl.when(use_col)
-            def _():
-                o_ref[...] -= dot(abuf[lk_at, :, rows], xcol[lk_at, rows, :])
+                send_all(to_col, tile, tile, col_send.at[lk_at], col_recv.at[lk_at, p])
+
+                @pl.when(use_col)
+                def _():
+                    o_ref[...] -= dot(abuf[lk_at, :, rows], xcol[lk_at, rows, :])
 
         return carry
 

time: 152 us -> 146 us (0.961)
  the two profiles are of different devices: /device:TPU:243 before, /device:TPU:2 now
where the time goes in v4:
time: 146 us
  Pallas kernels  138 us (95%)
  local copies, waits for them, and re-layouts  7.72 us (5%)
    pallas_call x1, Pallas kernels, per_device(): pl.pallas_call(kernel, out_shape=jax.ShapeDtypeStruct((size, size), F32),...  138 us
    unnamed x15, local copies, waits for them, and re-layouts  7.72 us

profile of v4, /device:TPU:2, one launch (start us, length us, event | category | flops | bytes accessed | tf_op | source)
XLA Modules:
  0.0 145.9 jit_solution(1257767999309932648)
XLA Ops:
  0.0 0.0 copy-start.5
  0.0 0.7 copy-done.5
  0.7 0.0 copy-start
  0.7 1.2 copy-done
  1.9 0.0 copy-start.1
  1.9 1.0 copy-done.1
  3.0 0.0 copy-start.2
  3.0 1.0 copy-done.2
  4.0 0.0 copy-start.3
  4.0 1.0 copy-done.3
  5.0 0.0 copy-start.4
  5.0 1.0 copy-done.4
  6.1 0.0 copy-start.6
  6.1 0.7 copy-done.6
  6.8 138.2 %sylvester.1 = f32[512,512]{1,0:T(8,128)S(1)} custom-call(f32[512,512]{1,0:T(8,128)S(1)} %copy-done, bf16[512,512]{1,0:T(8,128)(2,1)S(1)} %copy-done.1, bf16[512,512]{1,0:T(8,128)(2,1)S(1)} %copy-done.2, bf16[512,512]{1,0:T(8,128)(2,1)S(1)} %copy-done.3, bf16[512,512]{1,0:T(8,128)(2,1)S(1)} %copy-done.4, f32[1,512]{1,0:T(1,128)S(1)} %bitcast.2, ...), custom_call_target="tpu_custom_call" | custom-call | tf_op jit(solution)/shard_map/sylvester/pallas_call | solution.py:336
  145.0 1.0 copy.9
Async XLA Ops:
  0.0 0.7 copy-start.5
  0.7 1.2 copy-start
  1.9 1.0 copy-start.1
  3.0 1.0 copy-start.2
  4.0 1.0 copy-start.3
  5.0 1.0 copy-start.4
  6.1 0.7 copy-start.6

commit v5 on v4

--- a/solution.py
+++ b/solution.py
@@ -7,7 +7,7 @@
 
 STEPS = 8
 SIDE = 16
-CHUNKS = 4
+CHUNKS = 8
 MESH = pl.DeviceIdType.MESH
 BF16 = jnp.bfloat16
 F32 = jnp.float32
@@ -92,6 +92,13 @@
             pl.semaphore_signal(barrier, inc=1, device_id=(row, other), device_id_type=MESH)
 
         count = count + hit.astype(jnp.int32)
+    for load in loads:
+        load.wait()
+    ut[...] = u_ref[...].astype(F32).T.astype(BF16)
+    vt[...] = v_ref[...].astype(F32).T.astype(BF16)
+    sums = jnp.broadcast_to(al_ref[...], (size, size)).T + jnp.broadcast_to(bl_ref[...], (size, size))
+    inv[...] = 1.0 / sums
+
     pl.semaphore_wait(barrier, count)
 
     def a_children(t):
@@ -204,13 +211,6 @@
     @pl.when(is_a_source & (t_own != 5) & (t_own != 7) & (lag > t_own + 1))
     def _():
         pl.semaphore_signal(token, inc=1, device_id=(row, col - 1), device_id_type=MESH)
-
-    for load in loads:
-        load.wait()
-    ut[...] = u_ref[...].astype(F32).T.astype(BF16)
-    vt[...] = v_ref[...].astype(F32).T.astype(BF16)
-    sums = jnp.broadcast_to(al_ref[...], (size, size)).T + jnp.broadcast_to(bl_ref[...], (size, size))
-    inv[...] = 1.0 / sums
 
     def relay(condition, children, buffer, recvs, sends):
         @pl.when(condition)
@@ -348,7 +348,7 @@
             pltpu.SemaphoreType.REGULAR,
         ],
         compiler_params=pltpu.CompilerParams(
-            collective_id=0, has_side_effects=True, vmem_limit_bytes=48 << 20
+            collective_id=0, has_side_effects=True, vmem_limit_bytes=67043328
         ),
         name="sylvester",
     )(

time: 146 us -> 140 us (0.959)
  local copies, waits for them, and re-layouts: 7.72 us -> 2.26 us
    unnamed x15 -> x1, local copies, waits for them, and re-layouts: 7.72 us -> 2.26 us
where the time goes in v5:
time: 140 us
  Pallas kernels  137 us (98%)
  local copies, waits for them, and re-layouts  2.26 us (2%)
    pallas_call x1, Pallas kernels, per_device(): pl.pallas_call(kernel, out_shape=jax.ShapeDtypeStruct((size, size), F32),...  137 us

profile of v5, /device:TPU:2, one launch (start us, length us, event | category | flops | bytes accessed | tf_op | source)
XLA Modules:
  0.0 139.7 jit_solution(11163557514075205702)
XLA Ops:
  0.0 137.4 %sylvester.1 = f32[512,512]{1,0:T(8,128)} custom-call(f32[512,512]{1,0:T(8,128)} %c_any.1, bf16[512,512]{1,0:T(8,128)(2,1)} %a_any.1, bf16[512,512]{1,0:T(8,128)(2,1)} %b_any.1, bf16[512,512]{1,0:T(8,128)(2,1)} %u_any.1, bf16[512,512]{1,0:T(8,128)(2,1)} %v_any.1, f32[1,512]{1,0:T(1,128)} %bitcast.2, f32[1,512]{1,0:T(1,128)} %bitcast.3), custom_call_target="tpu_custom_call" | custom-call | tf_op jit(solution)/shard_map/sylvester/pallas_call | solution.py:336
  137.4 2.3 %copy.9 = f32[512,512]{1,0:T(8,128)} copy(f32[512,512]{1,0:T(8,128)} %sylvester.1) | data formatting | bytes 2097152

commit v6 on v5

--- a/solution.py
+++ b/solution.py
@@ -47,6 +47,7 @@
     size = o_ref.shape[0]
     part = size // CHUNKS
     parts = [pl.ds(p * part, part) for p in range(CHUNKS)]
+    large = [pl.ds(2 * p * part, 2 * part) for p in range(CHUNKS // 2)]
 
     def row_of(x_to, y_to):
         return ((y_to + 4) % 4) * 4 + (x_to + 4) % 4
@@ -181,7 +182,7 @@
 
     is_b_source = (row < STEPS) & (col > row)
     b_own = jnp.minimum(row, STEPS - 1)
-    for p, rows in enumerate(parts):
+    for p, rows in enumerate(large):
         send_all(
             b_children(b_own), b_any.at[rows], bbuf.at[b_own, rows], b_send.at[b_own],
             b_recv.at[b_own, p], is_b_source,
@@ -194,7 +195,7 @@
         copy(
             a_any.at[rows], abuf.at[t_own, rows], a_first.at[p], a_recv.at[t_own, p], row, a_target
         )
-        for p, rows in enumerate(parts)
+        for p, rows in enumerate(large)
     ]
 
     @pl.when(is_a_source & (t_own != 0) & (t_own != 6))
@@ -212,10 +213,10 @@
     def _():
         pl.semaphore_signal(token, inc=1, device_id=(row, col - 1), device_id_type=MESH)
 
-    def relay(condition, children, buffer, recvs, sends):
+    def relay(condition, children, buffer, recvs, sends, pieces=large):
         @pl.when(condition)
         def _():
-            for p, rows in enumerate(parts):
+            for p, rows in enumerate(pieces):
                 tile = buffer.at[rows]
                 received(tile, recvs.at[p])
                 send_all(children, tile, tile, sends, recvs.at[p])
@@ -276,18 +277,18 @@
                     to_row, src, xrow.at[k_at, rows], row_send.at[k_at], row_recv.at[k_at, p]
                 )
 
-        relay(from_row, to_row, xrow.at[k_at], row_recv.at[k_at], row_send.at[k_at])
+        relay(from_row, to_row, xrow.at[k_at], row_recv.at[k_at], row_send.at[k_at], parts)
 
         @pl.when(from_row)
         def _():
-            for p, rows in enumerate(parts):
+            for p, rows in enumerate(large):
                 received(bbuf.at[k_at, rows], b_recv.at[k_at, p])
             for p, rows in enumerate(parts):
                 o_ref[rows, :] -= dot(xrow[k_at, rows, :], bbuf[k_at])
 
         @pl.when(use_col & ~even)
         def _():
-            for p, rows in enumerate(parts):
+            for p, rows in enumerate(large):
                 received(abuf.at[lk_at, rows], a_recv.at[lk_at, p])
 
         @pl.when(from_col)

time: 140 us -> 140 us (level)
  no operation moved by 1% of the time
where the time goes in v6:
time: 140 us
  Pallas kernels  137 us (98%)
  local copies, waits for them, and re-layouts  2.26 us (2%)
    pallas_call x1, Pallas kernels, per_device(): pl.pallas_call(kernel, out_shape=jax.ShapeDtypeStruct((size, size), F32),...  137 us

profile of v6, /device:TPU:2, one launch (start us, length us, event | category | flops | bytes accessed | tf_op | source)
XLA Modules:
  0.0 139.7 jit_solution(12345124904268024014)
XLA Ops:
  0.0 137.4 %sylvester.1 = f32[512,512]{1,0:T(8,128)} custom-call(f32[512,512]{1,0:T(8,128)} %c_any.1, bf16[512,512]{1,0:T(8,128)(2,1)} %a_any.1, bf16[512,512]{1,0:T(8,128)(2,1)} %b_any.1, bf16[512,512]{1,0:T(8,128)(2,1)} %u_any.1, bf16[512,512]{1,0:T(8,128)(2,1)} %v_any.1, f32[1,512]{1,0:T(1,128)} %bitcast.2, f32[1,512]{1,0:T(1,128)} %bitcast.3), custom_call_target="tpu_custom_call" | custom-call | tf_op jit(solution)/shard_map/sylvester/pallas_call | solution.py:337
  137.4 2.3 %copy.9 = f32[512,512]{1,0:T(8,128)} copy(f32[512,512]{1,0:T(8,128)} %sylvester.1) | data formatting | bytes 2097152
